TPU v7x, 32 devices: a whole 2x2x4 slice. The times are simulated.
32 devices in a mesh: rows: 4 (over y, core), cols: 8 (over z, x).
Axes of the slice: x: 2, y: 2, z: 4, core: 2. Of those that a mesh axis runs over, the one named last changes fastest.
Arguments:
- costs: bfloat16 [4, 8, 24, 256, 256], P('rows', 'cols'), may hold values from -210 to 8
- block_rows: int32 [4, 8, 24], P('rows', 'cols'), may hold values from 0 to 7, as said below
- block_cols: int32 [4, 8, 24], P('rows', 'cols'), may hold values from 0 to 63, as said below
- live: int32 [4, 8], P('rows', 'cols'), may hold values from 16 to 24, as said below
- log_source: float32 [8192], P('rows'), may hold values from -6 to 6
- log_target: float32 [131072], P('cols'), may hold values from -6 to 6
Outputs:
- source_potential: float32 [8192], P('rows')
- target_potential: float32 [131072], P('cols')
Inputs may be any that keep to these rules, and one draw needn't show every extreme that they name: `block_rows`: row blocks are local to a device's 8 blocks of source cells. `block_cols`: column blocks are local to a device's 64 blocks of target cells. Every source cell and every target cell lies in some live block. `live`: live counts differ from device to device; some device uses all 24 slots.
All inputs are finite; a program needn't handle non-finite values.
Results may differ from a plain program's by a relative error of at most 0.0003.
Values sent between devices are 32-bit elements; how exact they have to be, the bound alone decides.
A program may use at most 64 MiB of HBM per device.

v0:
```python
import jax
import jax.numpy as jnp
from jax import lax
from jax.sharding import PartitionSpec as P

ITERS = 3
NEG = -1e30


def combined_all(value, axis, combine):
    everything = jax.tree.map(lambda part: lax.all_gather(part, axis), value)
    first = jax.tree.map(lambda part: part[0], everything)

    def hop(k, so_far):
        return combine(so_far, jax.tree.map(lambda part: part[k], everything))

    return lax.fori_loop(1, lax.axis_size(axis), hop, first)


def combine(first, second):
    top_a, tot_a = first
    top_b, tot_b = second
    top = jnp.maximum(top_a, top_b)
    return (top, tot_a * jnp.exp(top_a - top) + tot_b * jnp.exp(top_b - top))


def block_reduce(slot_top, score_fn, blocks_of, blocks, valid):
    select = (blocks_of[:, None] == jnp.arange(blocks, dtype=jnp.int32)[None, :]) & valid[:, None]
    block_top = jnp.max(jnp.where(select[:, :, None], slot_top[:, None, :], NEG), axis=0)
    own_top = jnp.max(jnp.where(select[:, :, None], block_top[None, :, :], NEG), axis=1)
    own_top = jnp.where(valid[:, None], own_top, 0.0)
    sums = score_fn(own_top)
    sums = jnp.where(valid[:, None], sums, 0.0)
    total = jnp.sum(jnp.where(select[:, :, None], sums[:, None, :], 0.0), axis=0)
    return (block_top.reshape(-1), total.reshape(-1))


def row_partial(tiles, rows_blk, cols_blk, valid, target_pot, row_blocks):
    width = tiles.shape[-1]
    pieces = target_pot.reshape(-1, width)[cols_blk]
    score = pieces[:, None, :] - tiles.astype(jnp.float32)
    slot_top = jnp.max(score, axis=2)

    def row_summed(own_top):
        return jnp.sum(jnp.exp(score - own_top[:, :, None]), axis=2)

    return block_reduce(slot_top, row_summed, rows_blk, row_blocks, valid)


def col_partial(tiles, rows_blk, cols_blk, valid, source_pot, col_blocks):
    width = tiles.shape[-1]
    pieces = source_pot.reshape(-1, width)[rows_blk]
    score = pieces[:, :, None] - tiles.astype(jnp.float32)
    slot_top = jnp.max(score, axis=1)

    def col_summed(own_top):
        return jnp.sum(jnp.exp(score - own_top[:, None, :]), axis=1)

    return block_reduce(slot_top, col_summed, cols_blk, col_blocks, valid)


def per_device(costs, block_rows, block_cols, live, log_source, log_target):
    tiles = costs[0, 0]
    rows_blk = block_rows[0, 0]
    cols_blk = block_cols[0, 0]
    count = live[0, 0]
    width = tiles.shape[-1]
    valid = jnp.arange(tiles.shape[0], dtype=jnp.int32) < count
    src_len = log_source.shape[0]
    tgt_len = log_target.shape[0]
    row_blocks = src_len // width
    col_blocks = tgt_len // width
    target_pot = jnp.zeros((tgt_len,), jnp.float32)
    source_pot = jnp.zeros((src_len,), jnp.float32)
    for sweep in range(ITERS):
        top, total = row_partial(tiles, rows_blk, cols_blk, valid, target_pot, row_blocks)
        common = lax.pmax(top, "cols")
        total = lax.psum(total * jnp.exp(top - common), "cols")
        top = common
        source_pot = log_source - (top + jnp.log(total))
        col_top, col_tot = col_partial(tiles, rows_blk, cols_blk, valid, source_pot, col_blocks)
        col_top, col_tot = combined_all((col_top, col_tot), "rows", combine)
        target_pot = log_target - (col_top + jnp.log(col_tot))
    return (source_pot, target_pot)


def solution(mesh):
    in_specs = (
        P("rows", "cols", None, None, None),
        P("rows", "cols", None),
        P("rows", "cols", None),
        P("rows", "cols"),
        P("rows"),
        P("cols"),
    )
    out_specs = (P("rows"), P("cols"))
    return jax.shard_map(
        per_device, mesh=mesh, in_specs=in_specs, out_specs=out_specs, check_vma=False
    )
```

profile of v0, /device:TPU:0, one launch (start us, length us, event | category | flops | bytes accessed | tf_op | source)
XLA Modules:
  0.0 195.3 jit_solution(16827550042038354003)
XLA Ops:
  1.4 0.9 fusion.24
  2.3 0.7 fusion.26
  3.0 0.6 gather_fusion
  3.6 2.8 %fusion.1 = f32[24,256]{1,0:T(8,128)S(1)} fusion(bf16[1,1,24,256,256]{4,3,2,1,0:T(8,128)(2,1)} %param.12, f32[24,256]{1,0:T(8,128)S(1)} %gather_fusion), kind=kLoop, calls=%fused_computation.22 | loop fusion | flops 4712448 | bytes 3194880 | tf_op jit(solution)/shard_map/reduce_max | solution.py:42
  6.7 2.1 %fusion.23 = f32[24,256]{1,0:T(8,128)S(1)} fusion(bf16[1,1,24,256,256]{4,3,2,1,0:T(8,128)(2,1)S(1)} %copy-done, f32[24,256]{1,0:T(8,128)S(1)} %broadcast_select_fusion.11, f32[24,256]{1,0:T(8,128)S(1)} %gather_fusion), kind=kLoop, calls=%fused_computation.44 | loop fusion | flops 6285312 | bytes 3219456 | tf_op jit(solution)/shard_map/reduce_sum | solution.py:45
  9.0 23.4 %pmax.21 = f32[2048]{0:T(1024)S(1)} all-reduce(f32[2048]{0:T(1024)S(1)} %bitcast.98), channel_id=1, replica_groups=mesh['rows'=4,'cols'=8] {'cols'}, use_global_device_ids=true, to_apply=%region_2.3 | all-reduce | flops 2048 | bytes 16384 | tf_op jit(solution)/shard_map/pmax | solution.py:77
  32.4 17.4 %psum.21 = f32[2048]{0:T(1024)S(1)} all-reduce(f32[2048]{0:T(1024)S(1)} %exponential_multiply_fusion.2), channel_id=1, replica_groups=mesh['rows'=4,'cols'=8] {'cols'}, use_global_device_ids=true, to_apply=%region_6.7 | all-reduce | flops 2048 | bytes 16384 | tf_op jit(solution)/shard_map/psum | solution.py:78
  49.9 0.6 gather_fusion.1
  50.5 1.0 fusion.3
  52.4 1.6 fusion.21
  54.4 5.8 %all-gather.1 = f32[4,1,16384]{2,1,0:T(1,128)S(1)} all-gather(f32[1,1,16384]{2,1,0:T(1,128)S(1)} %reshape.438), channel_id=1, replica_groups=mesh['rows'=4,'cols'=8] {'rows'}, dimensions={0}, use_global_device_ids=true | all-gather | bytes 327680 | tf_op jit(solution)/shard_map/all_gather | solution.py:11
  60.4 0.7 reshape.436
  61.0 6.0 %all-gather = f32[4,1,16384]{2,1,0:T(1,128)S(1)} all-gather(f32[1,1,16384]{2,1,0:T(1,128)} %reshape.436), channel_id=1, replica_groups=mesh['rows'=4,'cols'=8] {'rows'}, dimensions={0}, use_global_device_ids=true | all-gather | bytes 327680 | tf_op jit(solution)/shard_map/all_gather | solution.py:11
  67.1 0.9 copy.31
  68.0 3.6 %while.51 = (s32[]{:T(128)}, f32[16384]{0:T(1024)S(1)}, f32[16384]{0:T(1024)S(1)}, f32[4,16384]{1,0:T(4,128)}, f32[4,16384]{1,0:T(4,128)S(1)}, /*index=5*/s32[]{:T(128)}, s32[]{:T(128)}, s32[]{:T(128)}) while((s32[]{:T(128)}, f32[16384]{0:T(1024)S(1)}, f32[16384]{0:T(1024)S(1)}, f32[4,16384]{1,0:T(4,128)}, f32[4,16384]{1,0:T(4,128)S(1)}, ...), condition=%wide.region_13.14_spmd, body=%wide.region_12.13_spmd.sunk | while | flops 98309 | bytes 655491 | solution.py:17
  68.0 1.1 constant_dynamic-slice_fusion.9
  69.2 1.1 constant_dynamic-slice_fusion.9
  70.4 1.1 constant_dynamic-slice_fusion.9
  71.6 0.9 add_subtract_fusion.2
  72.5 0.6 gather_fusion.2
  73.1 1.0 fusion.5
  74.4 2.1 %fusion.19 = f32[24,256]{1,0:T(8,128)S(1)} fusion(bf16[1,1,24,256,256]{4,3,2,1,0:T(8,128)(2,1)S(1)} %copy-done, f32[24,256]{1,0:T(8,128)S(1)} %broadcast_select_fusion.7, f32[24,256]{1,0:T(8,128)S(1)} %gather_fusion.2), kind=kLoop, calls=%fused_computation.40 | loop fusion | flops 6285312 | bytes 3219456 | tf_op jit(solution)/shard_map/reduce_sum | solution.py:45
  76.7 19.4 %pmax.22 = f32[2048]{0:T(1024)S(1)} all-reduce(f32[2048]{0:T(1024)S(1)} %bitcast.100), channel_id=1, replica_groups=mesh['rows'=4,'cols'=8] {'cols'}, use_global_device_ids=true, to_apply=%region_16.17 | all-reduce | flops 2048 | bytes 16384 | tf_op jit(solution)/shard_map/pmax | solution.py:77
  96.1 17.4 %psum.22 = f32[2048]{0:T(1024)S(1)} all-reduce(f32[2048]{0:T(1024)S(1)} %exponential_multiply_fusion.1), channel_id=1, replica_groups=mesh['rows'=4,'cols'=8] {'cols'}, use_global_device_ids=true, to_apply=%region_20.21 | all-reduce | flops 2048 | bytes 16384 | tf_op jit(solution)/shard_map/psum | solution.py:78
  113.5 0.7 gather_fusion.3
  114.2 1.0 fusion.7
  116.0 1.6 fusion.17
  118.0 5.8 %all-gather.3 = f32[4,1,16384]{2,1,0:T(1,128)S(1)} all-gather(f32[1,1,16384]{2,1,0:T(1,128)S(1)} %reshape.442), channel_id=1, replica_groups=mesh['rows'=4,'cols'=8] {'rows'}, dimensions={0}, use_global_device_ids=true | all-gather | bytes 327680 | tf_op jit(solution)/shard_map/all_gather | solution.py:11
  124.0 0.7 reshape.440
  124.7 6.2 %all-gather.2 = f32[4,1,16384]{2,1,0:T(1,128)S(1)} all-gather(f32[1,1,16384]{2,1,0:T(1,128)} %reshape.440), channel_id=1, replica_groups=mesh['rows'=4,'cols'=8] {'rows'}, dimensions={0}, use_global_device_ids=true | all-gather | bytes 327680 | tf_op jit(solution)/shard_map/all_gather | solution.py:11
  130.9 0.9 copy.29
  131.8 3.6 %while.52 = (s32[]{:T(128)}, f32[16384]{0:T(1024)S(1)}, f32[16384]{0:T(1024)S(1)}, f32[4,16384]{1,0:T(4,128)}, f32[4,16384]{1,0:T(4,128)S(1)}, /*index=5*/s32[]{:T(128)}, s32[]{:T(128)}, s32[]{:T(128)}) while((s32[]{:T(128)}, f32[16384]{0:T(1024)S(1)}, f32[16384]{0:T(1024)S(1)}, f32[4,16384]{1,0:T(4,128)}, f32[4,16384]{1,0:T(4,128)S(1)}, ...), condition=%wide.region_27.28_spmd, body=%wide.region_26.27_spmd.sunk | while | flops 98309 | bytes 655491 | solution.py:17
  131.8 1.1 constant_dynamic-slice_fusion.10
  132.9 1.1 constant_dynamic-slice_fusion.10
  134.2 1.1 constant_dynamic-slice_fusion.10
  135.3 0.9 add_subtract_fusion.1
  136.2 0.6 gather_fusion.4
  136.8 1.0 fusion.9
  138.2 2.1 %fusion.15 = f32[24,256]{1,0:T(8,128)S(1)} fusion(bf16[1,1,24,256,256]{4,3,2,1,0:T(8,128)(2,1)S(1)} %copy-done, f32[24,256]{1,0:T(8,128)S(1)} %broadcast_select_fusion.3, f32[24,256]{1,0:T(8,128)S(1)} %gather_fusion.4), kind=kLoop, calls=%fused_computation.36 | loop fusion | flops 6285312 | bytes 3219456 | tf_op jit(solution)/shard_map/reduce_sum | solution.py:45
  140.4 19.4 %pmax.23 = f32[2048]{0:T(1024)S(1)} all-reduce(f32[2048]{0:T(1024)S(1)} %bitcast.102), channel_id=1, replica_groups=mesh['rows'=4,'cols'=8] {'cols'}, use_global_device_ids=true, to_apply=%region_30.31 | all-reduce | flops 2048 | bytes 16384 | tf_op jit(solution)/shard_map/pmax | solution.py:77
  159.9 17.4 %psum.23 = f32[2048]{0:T(1024)S(1)} all-reduce(f32[2048]{0:T(1024)S(1)} %exponential_multiply_fusion), channel_id=1, replica_groups=mesh['rows'=4,'cols'=8] {'cols'}, use_global_device_ids=true, to_apply=%region_34.35 | all-reduce | flops 2048 | bytes 16384 | tf_op jit(solution)/shard_map/psum | solution.py:78
  177.3 0.7 gather_fusion.5
  178.0 1.0 fusion.11
  179.8 1.6 fusion.13
  181.8 5.8 %all-gather.5 = f32[4,1,16384]{2,1,0:T(1,128)S(1)} all-gather(f32[1,1,16384]{2,1,0:T(1,128)S(1)} %reshape.446), channel_id=1, replica_groups=mesh['rows'=4,'cols'=8] {'rows'}, dimensions={0}, use_global_device_ids=true | all-gather | bytes 327680 | tf_op jit(solution)/shard_map/all_gather | solution.py:11
  187.9 5.9 %all-gather.4 = f32[4,1,16384]{2,1,0:T(1,128)S(1)} all-gather(f32[1,1,16384]{2,1,0:T(1,128)S(1)} %reshape.444), channel_id=1, replica_groups=mesh['rows'=4,'cols'=8] {'rows'}, dimensions={0}, use_global_device_ids=true | all-gather | bytes 327680 | tf_op jit(solution)/shard_map/all_gather | solution.py:11
  193.9 0.7 while.53
  194.6 0.6 add_subtract_fusion
  (97 shorter events, 6.8 us)
Async XLA Ops:
  0.6 6.1 %copy-start = (bf16[1,1,24,256,256]{4,3,2,1,0:T(8,128)(2,1)S(1)}, bf16[1,1,24,256,256]{4,3,2,1,0:T(8,128)(2,1)}, u32[]{:S(2)}) copy-start(bf16[1,1,24,256,256]{4,3,2,1,0:T(8,128)(2,1)} %param.12) | copy-start | bytes 9437188
  3.6 46.2 %copy-start.2 = (f32[2048]{0:T(1024)S(1)}, f32[2048]{0:T(1024)}, u32[]{:S(2)}) copy-start(f32[2048]{0:T(1024)} %param.16) | copy-start | bytes 24580
  3.6 46.3 %copy-start.7 = (s32[1,1,24]{2,1,0:T(1,128)S(1)}, s32[1,1,24]{2,1,0:T(1,128)}, u32[]{:S(2)}) copy-start(s32[1,1,24]{2,1,0:T(1,128)} %param.13) | copy-start | bytes 292
  6.7 44.8 %copy-start.8 = (s32[1,1,24]{2,1,0:T(1,128)S(1)}, s32[1,1,24]{2,1,0:T(1,128)}, u32[]{:S(2)}) copy-start(s32[1,1,24]{2,1,0:T(1,128)} %param.14) | copy-start | bytes 292
  49.9 1.7 copy-start.6
  73.0 40.4 %copy-start.3 = (f32[2048]{0:T(1024)S(1)}, f32[2048]{0:T(1024)}, u32[]{:S(2)}) copy-start(f32[2048]{0:T(1024)} %param.16) | copy-start | bytes 24580
  136.8 40.4 %copy-start.4 = (f32[2048]{0:T(1024)S(1)}, f32[2048]{0:T(1024)}, u32[]{:S(2)}) copy-start(f32[2048]{0:T(1024)} %param.16) | copy-start | bytes 24580
  177.3 4.1 %copy-start.5 = (f32[2048]{0:T(1024)}, f32[2048]{0:T(1024)S(1)}, u32[]{:S(2)}) copy-start(f32[2048]{0:T(1024)S(1)} %add_subtract_fusion.3) | copy-start | bytes 24580
  181.4 13.2 %copy-start.1 = (f32[16384]{0:T(1024)S(1)}, f32[16384]{0:T(1024)}, u32[]{:S(2)}) copy-start(f32[16384]{0:T(1024)} %param.17) | copy-start | bytes 196612
where the time goes:
time: 196 us; the launch traced here: 195 us
  blocking collectives  150 us (77%)
  other arithmetic  28.1 us (14%)
  local copies, waits for them, and re-layouts  15.1 us (8%)
  between operations  2.1 us (1%)
    pmax x3, blocking collectives, per_device(): common = lax.pmax(top, 'cols')  62.2 us
    psum x3, blocking collectives, per_device(): total = lax.psum(total * jnp.exp(top - common), 'cols')  52.1 us
    all_gather x6, blocking collectives, combined_all(): everything = jax.tree.map(lambda part: lax.all_gather(part, axis), value)  35.5 us
    dynamic_slice x9, local copies, waits for them, and re-layouts, hop(): return combine(so_far, jax.tree.map(lambda part: part[k], everything))  7.07 us
    reduce_sum x3, other arithmetic, row_summed(): return jnp.sum(jnp.exp(score - own_top[:, :, None]), axis=2)  6.26 us
    reduce_sum x3, other arithmetic, col_summed(): return jnp.sum(jnp.exp(score - own_top[:, None, :]), axis=1)  4.79 us
    reduce_max x3, other arithmetic, row_partial(): slot_top = jnp.max(score, axis=2)  4.78 us
    unnamed x36, local copies, waits for them, and re-layouts  4.16 us

commit v1 on v0

--- a/solution.py
+++ b/solution.py
@@ -2,6 +2,7 @@
 import jax.numpy as jnp
 from jax import lax
 from jax.sharding import PartitionSpec as P
+from jax.lax import all_gather
 
 ITERS = 3
 NEG = -1e30
@@ -75,7 +76,7 @@
     for sweep in range(ITERS):
         top, total = row_partial(tiles, rows_blk, cols_blk, valid, target_pot, row_blocks)
         common = lax.pmax(top, "cols")
-        total = lax.psum(total * jnp.exp(top - common), "cols")
+        total = jnp.sum(all_gather(total * jnp.exp(top - common), "cols"), axis=0)
         top = common
         source_pot = log_source - (top + jnp.log(total))
         col_top, col_tot = col_partial(tiles, rows_blk, cols_blk, valid, source_pot, col_blocks)

time: 196 us -> 233 us (1.19)
  blocking collectives: 150 us -> 187 us
    all_gather x0 -> x3, blocking collectives: none -> 91.6 us  [per_device(): total = jnp.sum(all_gather(total * jnp.exp(top - common), 'cols'), axis=0)]
    psum x3 -> x0, blocking collectives: 52.1 us -> none  [per_device(): total = lax.psum(total * jnp.exp(top - common), 'cols')]
where the time goes in v1:
time: 233 us
  blocking collectives  187 us (80%)
  other arithmetic  28.2 us (12%)
  local copies, waits for them, and re-layouts  15.2 us (7%)
    all_gather x3, blocking collectives, per_device(): total = jnp.sum(all_gather(total * jnp.exp(top - common), 'cols'), axis=0)  91.6 us
    pmax x3, blocking collectives, per_device(): common = lax.pmax(top, 'cols')  60.2 us
    all_gather x6, blocking collectives, combined_all(): everything = jax.tree.map(lambda part: lax.all_gather(part, axis), value)  35.5 us
    dynamic_slice x9, local copies, waits for them, and re-layouts, hop(): return combine(so_far, jax.tree.map(lambda part: part[k], everything))  7.07 us
    reduce_sum x3, other arithmetic, row_summed(): return jnp.sum(jnp.exp(score - own_top[:, :, None]), axis=2)  6.26 us
    reduce_sum x3, other arithmetic, col_summed(): return jnp.sum(jnp.exp(score - own_top[:, None, :]), axis=1)  4.79 us
    reduce_max x3, other arithmetic, row_partial(): slot_top = jnp.max(score, axis=2)  4.78 us

profile of v1, /device:TPU:0, one launch (start us, length us, event | category | flops | bytes accessed | tf_op | source)
XLA Modules:
  0.0 232.9 jit_solution(17026967554196938582)
XLA Ops:
  1.4 0.9 fusion.24
  2.3 0.7 fusion.26
  3.0 0.6 gather_fusion
  3.6 2.8 %fusion.1 = f32[24,256]{1,0:T(8,128)S(1)} fusion(bf16[1,1,24,256,256]{4,3,2,1,0:T(8,128)(2,1)} %param.12, f32[24,256]{1,0:T(8,128)S(1)} %gather_fusion), kind=kLoop, calls=%fused_computation.22 | loop fusion | flops 4712448 | bytes 3194880 | tf_op jit(solution)/shard_map/reduce_max | solution.py:43
  6.7 2.1 fusion.23
  9.0 23.4 %pmax.21 = f32[2048]{0:T(1024)S(1)} all-reduce(f32[2048]{0:T(1024)S(1)} %bitcast.98), channel_id=1, replica_groups=mesh['rows'=4,'cols'=8] {'cols'}, use_global_device_ids=true, to_apply=%region_2.3 | all-reduce | flops 2048 | bytes 16384 | tf_op jit(solution)/shard_map/pmax | solution.py:78
  32.4 30.5 %all-gather = f32[16384]{0:T(1024)S(1)} all-gather(f32[2048]{0:T(1024)S(1)} %exponential_multiply_fusion.2), channel_id=2, replica_groups=mesh['rows'=4,'cols'=8] {'cols'}, dimensions={0}, use_global_device_ids=true | all-gather | bytes 73728 | tf_op jit(solution)/shard_map/all_gather | solution.py:79
  63.1 0.6 gather_fusion.1
  63.7 1.0 fusion.3
  65.6 1.6 fusion.21
  67.6 5.8 %all-gather.4 = f32[4,1,16384]{2,1,0:T(1,128)S(1)} all-gather(f32[1,1,16384]{2,1,0:T(1,128)S(1)} %reshape.441), channel_id=1, replica_groups=mesh['rows'=4,'cols'=8] {'rows'}, dimensions={0}, use_global_device_ids=true | all-gather | bytes 327680 | tf_op jit(solution)/shard_map/all_gather | solution.py:12
  73.5 0.7 reshape.439
  74.2 6.0 %all-gather.3 = f32[4,1,16384]{2,1,0:T(1,128)S(1)} all-gather(f32[1,1,16384]{2,1,0:T(1,128)} %reshape.439), channel_id=1, replica_groups=mesh['rows'=4,'cols'=8] {'rows'}, dimensions={0}, use_global_device_ids=true | all-gather | bytes 327680 | tf_op jit(solution)/shard_map/all_gather | solution.py:12
  80.3 0.9 copy.31
  81.2 3.6 %while.51 = (s32[]{:T(128)}, f32[16384]{0:T(1024)S(1)}, f32[16384]{0:T(1024)S(1)}, f32[4,16384]{1,0:T(4,128)}, f32[4,16384]{1,0:T(4,128)S(1)}, /*index=5*/s32[]{:T(128)}, s32[]{:T(128)}, s32[]{:T(128)}) while((s32[]{:T(128)}, f32[16384]{0:T(1024)S(1)}, f32[16384]{0:T(1024)S(1)}, f32[4,16384]{1,0:T(4,128)}, f32[4,16384]{1,0:T(4,128)S(1)}, ...), condition=%wide.region_13.14_spmd, body=%wide.region_12.13_spmd.sunk | while | flops 98309 | bytes 655491 | solution.py:18
  81.2 1.1 constant_dynamic-slice_fusion.9
  82.4 1.1 constant_dynamic-slice_fusion.9
  83.6 1.1 constant_dynamic-slice_fusion.9
  84.8 0.9 add_subtract_fusion.2
  85.7 0.6 gather_fusion.2
  86.3 1.0 fusion.5
  87.6 2.1 fusion.19
  89.9 17.4 %pmax.22 = f32[2048]{0:T(1024)S(1)} all-reduce(f32[2048]{0:T(1024)S(1)} %bitcast.100), channel_id=1, replica_groups=mesh['rows'=4,'cols'=8] {'cols'}, use_global_device_ids=true, to_apply=%region_16.17 | all-reduce | flops 2048 | bytes 16384 | tf_op jit(solution)/shard_map/pmax | solution.py:78
  107.3 30.5 %all-gather.1 = f32[16384]{0:T(1024)S(1)} all-gather(f32[2048]{0:T(1024)S(1)} %exponential_multiply_fusion.1), channel_id=3, replica_groups=mesh['rows'=4,'cols'=8] {'cols'}, dimensions={0}, use_global_device_ids=true | all-gather | bytes 73728 | tf_op jit(solution)/shard_map/all_gather | solution.py:79
  137.9 0.7 gather_fusion.3
  138.6 1.0 fusion.7
  140.4 1.6 fusion.17
  142.4 5.8 %all-gather.6 = f32[4,1,16384]{2,1,0:T(1,128)S(1)} all-gather(f32[1,1,16384]{2,1,0:T(1,128)S(1)} %reshape.445), channel_id=1, replica_groups=mesh['rows'=4,'cols'=8] {'rows'}, dimensions={0}, use_global_device_ids=true | all-gather | bytes 327680 | tf_op jit(solution)/shard_map/all_gather | solution.py:12
  148.3 0.7 reshape.443
  149.0 6.2 %all-gather.5 = f32[4,1,16384]{2,1,0:T(1,128)S(1)} all-gather(f32[1,1,16384]{2,1,0:T(1,128)} %reshape.443), channel_id=1, replica_groups=mesh['rows'=4,'cols'=8] {'rows'}, dimensions={0}, use_global_device_ids=true | all-gather | bytes 327680 | tf_op jit(solution)/shard_map/all_gather | solution.py:12
  155.3 0.9 copy.29
  156.1 3.6 %while.52 = (s32[]{:T(128)}, f32[16384]{0:T(1024)S(1)}, f32[16384]{0:T(1024)S(1)}, f32[4,16384]{1,0:T(4,128)}, f32[4,16384]{1,0:T(4,128)S(1)}, /*index=5*/s32[]{:T(128)}, s32[]{:T(128)}, s32[]{:T(128)}) while((s32[]{:T(128)}, f32[16384]{0:T(1024)S(1)}, f32[16384]{0:T(1024)S(1)}, f32[4,16384]{1,0:T(4,128)}, f32[4,16384]{1,0:T(4,128)S(1)}, ...), condition=%wide.region_27.28_spmd, body=%wide.region_26.27_spmd.sunk | while | flops 98309 | bytes 655491 | solution.py:18
  156.1 1.1 constant_dynamic-slice_fusion.10
  157.3 1.1 constant_dynamic-slice_fusion.10
  158.5 1.1 constant_dynamic-slice_fusion.10
  159.7 0.9 add_subtract_fusion.1
  160.6 0.6 gather_fusion.4
  161.2 1.0 fusion.9
  162.5 2.1 fusion.15
  164.8 19.4 %pmax.23 = f32[2048]{0:T(1024)S(1)} all-reduce(f32[2048]{0:T(1024)S(1)} %bitcast.102), channel_id=1, replica_groups=mesh['rows'=4,'cols'=8] {'cols'}, use_global_device_ids=true, to_apply=%region_30.31 | all-reduce | flops 2048 | bytes 16384 | tf_op jit(solution)/shard_map/pmax | solution.py:78
  184.3 30.5 %all-gather.2 = f32[16384]{0:T(1024)S(1)} all-gather(f32[2048]{0:T(1024)S(1)} %exponential_multiply_fusion), channel_id=4, replica_groups=mesh['rows'=4,'cols'=8] {'cols'}, dimensions={0}, use_global_device_ids=true | all-gather | bytes 73728 | tf_op jit(solution)/shard_map/all_gather | solution.py:79
  214.9 0.7 gather_fusion.5
  215.6 1.0 fusion.11
  217.4 1.6 fusion.13
  219.4 5.8 %all-gather.8 = f32[4,1,16384]{2,1,0:T(1,128)S(1)} all-gather(f32[1,1,16384]{2,1,0:T(1,128)S(1)} %reshape.449), channel_id=1, replica_groups=mesh['rows'=4,'cols'=8] {'rows'}, dimensions={0}, use_global_device_ids=true | all-gather | bytes 327680 | tf_op jit(solution)/shard_map/all_gather | solution.py:12
  225.5 5.9 %all-gather.7 = f32[4,1,16384]{2,1,0:T(1,128)S(1)} all-gather(f32[1,1,16384]{2,1,0:T(1,128)S(1)} %reshape.447), channel_id=1, replica_groups=mesh['rows'=4,'cols'=8] {'rows'}, dimensions={0}, use_global_device_ids=true | all-gather | bytes 327680 | tf_op jit(solution)/shard_map/all_gather | solution.py:12
  231.5 0.7 while.53
  232.2 0.6 add_subtract_fusion
  (103 shorter events, 6.9 us)
Async XLA Ops:
  0.6 6.1 %copy-start = (bf16[1,1,24,256,256]{4,3,2,1,0:T(8,128)(2,1)S(1)}, bf16[1,1,24,256,256]{4,3,2,1,0:T(8,128)(2,1)}, u32[]{:S(2)}) copy-start(bf16[1,1,24,256,256]{4,3,2,1,0:T(8,128)(2,1)} %param.12) | copy-start | bytes 9437188
  3.6 59.4 %copy-start.2 = (f32[2048]{0:T(1024)S(1)}, f32[2048]{0:T(1024)}, u32[]{:S(2)}) copy-start(f32[2048]{0:T(1024)} %param.16) | copy-start | bytes 24580
  3.6 59.5 %copy-start.7 = (s32[1,1,24]{2,1,0:T(1,128)S(1)}, s32[1,1,24]{2,1,0:T(1,128)}, u32[]{:S(2)}) copy-start(s32[1,1,24]{2,1,0:T(1,128)} %param.13) | copy-start | bytes 292
  6.7 58.0 %copy-start.8 = (s32[1,1,24]{2,1,0:T(1,128)S(1)}, s32[1,1,24]{2,1,0:T(1,128)}, u32[]{:S(2)}) copy-start(s32[1,1,24]{2,1,0:T(1,128)} %param.14) | copy-start | bytes 292
  63.1 1.7 copy-start.6
  86.2 51.6 %copy-start.3 = (f32[2048]{0:T(1024)S(1)}, f32[2048]{0:T(1024)}, u32[]{:S(2)}) copy-start(f32[2048]{0:T(1024)} %param.16) | copy-start | bytes 24580
  161.2 53.6 %copy-start.4 = (f32[2048]{0:T(1024)S(1)}, f32[2048]{0:T(1024)}, u32[]{:S(2)}) copy-start(f32[2048]{0:T(1024)} %param.16) | copy-start | bytes 24580
  214.9 4.1 %copy-start.5 = (f32[2048]{0:T(1024)}, f32[2048]{0:T(1024)S(1)}, u32[]{:S(2)}) copy-start(f32[2048]{0:T(1024)S(1)} %add_subtract_fusion.3) | copy-start | bytes 24580
  219.0 13.2 %copy-start.1 = (f32[16384]{0:T(1024)S(1)}, f32[16384]{0:T(1024)}, u32[]{:S(2)}) copy-start(f32[16384]{0:T(1024)} %param.17) | copy-start | bytes 196612
